TPU v7x, 256 devices: a whole 4x4x8 slice. The times are simulated.
256 devices in a mesh: blk: 8 (over x_lo, y), freq: 32 (over x_hi, z, core).
Axes of the slice: x: 4 (x_hi: 2, x_lo: 2; x = x_hi * 2 + x_lo), y: 4, z: 8, core: 2. Of those that a mesh axis runs over, the one named last changes fastest.
Arguments:
- spectra: bfloat16 [2048, 2, 4096], P('blk', None, 'freq'), may hold values from -180 to 180
- pair_first: int32 [8, 8, 2048], P('blk'), may hold values from 0 to 255
- pair_second: int32 [8, 8, 2048], P('blk'), may hold values from 0 to 255
- pair_bin: int32 [8, 8, 2048], P('blk'), may hold values from 0 to 63, as said below
- bin_owner: int32 [64], replicated, may hold values from 0 to 7, as said below
Outputs:
- correlation: float32 [4096, 128], P('freq', 'blk')
Inputs may be any that keep to these rules, and one draw needn't show every extreme that they name: Each list pair_bin[a, r] is nondecreasing along its last dimension, starts with 0 and ends with 63. `bin_owner`: each block index owns at most 16 bins, and some index owns exactly 16.
All inputs are finite; a program needn't handle non-finite values.
Results may differ from a plain program's by a relative error of at most 0.0049.
Values may be sent and summed in bfloat16 or wider, within the bound.
No kernel may reach another device: no remote copies, remote signals or barrier semaphores. Data moves between devices by JAX's collectives and lax.ppermute only.
A program may use at most 64 MiB of HBM per device.

v0:
```python
import math
import jax
import jax.numpy as jnp
from jax import lax
from jax.sharding import PartitionSpec as P

F = 4096
NB = 64
PAIRS = 2048


def from_behind(x, axis, by):
    devices = lax.axis_size(axis)
    return lax.ppermute(x, axis, [(i, (i + by) % devices) for i in range(devices)])


def cross_stack(total, white, remote, first_rows, second_rows, bin_rows):
    left = white[first_rows].astype(jnp.float32)
    right = remote[second_rows].astype(jnp.float32)
    real_part = left[:, 0] * right[:, 0] + left[:, 1] * right[:, 1]
    imag_part = left[:, 1] * right[:, 0] - left[:, 0] * right[:, 1]
    cross = jnp.stack([real_part, imag_part], 1).astype(jnp.bfloat16)
    onehot = (bin_rows[None, :] == jnp.arange(NB, dtype=jnp.int32)[:, None]).astype(jnp.bfloat16)
    flat = cross.reshape(cross.shape[0], -1)
    return total + jnp.dot(onehot, flat, preferred_element_type=jnp.float32)


def lag_block(lag_rows, freq_rows, piece):
    phase = (lag_rows[:, None] * freq_rows[None, :] % F).astype(jnp.float32) * (2.0 * math.pi / F)
    line = jnp.dot(jnp.cos(phase), piece[:, 0, :].T, precision=lax.Precision.HIGHEST)
    return line - jnp.dot(jnp.sin(phase), piece[:, 1, :].T, precision=lax.Precision.HIGHEST)


def on_device(spectra, pair_first, pair_second, pair_bin, bin_owner):
    blocks = lax.axis_size("blk")
    freq_dev = spectra.shape[2]
    values = spectra.astype(jnp.float32)
    power = lax.psum(jnp.sum(values * values, axis=(1, 2)), "freq")
    rms = jnp.sqrt(power / (2 * F) + 1e-06)
    white = (values / rms[:, None, None]).astype(jnp.bfloat16)
    total = jnp.zeros((NB, 2 * freq_dev), jnp.float32)
    remote = white
    for step_count in range(blocks):
        if step_count > 0:
            remote = from_behind(remote, "blk", 1)
        total = cross_stack(
            total,
            white,
            remote,
            pair_first[0, step_count],
            pair_second[0, step_count],
            pair_bin[0, step_count],
        )
    partial_stack = total.reshape(NB, 2, freq_dev)
    slots_each = 2 * NB // blocks
    bins = jnp.arange(NB, dtype=jnp.int32)
    same = bin_owner[:, None] == bin_owner[None, :]
    lower = bins[None, :] < bins[:, None]
    rank = jnp.sum((same & lower).astype(jnp.int32), axis=1)
    slot = bin_owner * slots_each + rank
    totals = lax.psum(partial_stack, "blk")
    mine = lax.axis_index("blk")
    wanted = mine * slots_each + jnp.arange(slots_each, dtype=jnp.int32)
    select = (slot[None, :] == wanted[:, None]).astype(jnp.float32)
    owned = jnp.einsum("sb,bcf->scf", select, totals, precision=lax.Precision.HIGHEST)
    freq_index = lax.axis_index("freq")
    scale = (F * PAIRS * blocks * blocks / NB) ** (-0.5)
    lag_rows = jnp.arange(freq_dev * lax.axis_size("freq"), dtype=jnp.int32)
    freq_rows = freq_index * freq_dev + jnp.arange(freq_dev, dtype=jnp.int32)
    line = lax.psum_scatter(
        lag_block(lag_rows, freq_rows, owned), "freq", scatter_dimension=0, tiled=True
    )
    return line * scale


def solution(mesh):
    return jax.shard_map(
        on_device,
        mesh=mesh,
        in_specs=(
            P("blk", None, "freq"),
            P("blk", None, None),
            P("blk", None, None),
            P("blk", None, None),
            P(),
        ),
        out_specs=P("freq", "blk"),
        check_vma=False,
    )
```

profile of v0, /device:TPU:8, one launch (start us, length us, event | category | flops | bytes accessed | tf_op | source)
XLA Modules:
  0.0 524.1 jit_solution(14951603235629611911)
XLA Ops:
  6.5 1.9 fusion.29
  8.5 72.8 %psum.14 = f32[256]{0:T(256)S(1)} all-reduce(f32[256]{0:T(256)S(1)} %fusion.29), channel_id=1, replica_groups=mesh['blk'=8,'freq'=32] {'freq'}, use_global_device_ids=true, to_apply=%region_2.0 | all-reduce | flops 256 | bytes 2048 | tf_op jit(solution)/shard_map/psum | solution.py:38
  85.5 7.1 %gather_fusion = bf16[2048,2,128]{2,1,0:T(2,128)(2,1)S(1)} fusion(bf16[256,2,128]{2,1,0:T(2,128)(2,1)S(1)} %fusion.30, s32[2048]{0:T(1024)S(1)} %broadcast_clamp_fusion.15), kind=kCustom, calls=%fused_computation | custom fusion | bytes 2105344 | tf_op jit(solution)/shard_map/gather | solution.py:18
  93.5 7.0 %gather_fusion.1 = bf16[2048,2,128]{2,1,0:T(2,128)(2,1)S(1)} fusion(bf16[256,2,128]{2,1,0:T(2,128)(2,1)S(1)} %fusion.30, s32[2048]{0:T(1024)S(1)} %broadcast_clamp_fusion.14), kind=kCustom, calls=%fused_computation.1 | custom fusion | bytes 2105344 | tf_op jit(solution)/shard_map/gather | solution.py:19
  102.4 3.3 add_convert_fusion.7
  105.7 2.4 pad_maximum_fusion
  109.1 7.0 %gather_fusion.2 = bf16[2048,2,128]{2,1,0:T(2,128)(2,1)S(1)} fusion(bf16[256,2,128]{2,1,0:T(2,128)(2,1)S(1)} %fusion.30, s32[2048]{0:T(1024)S(1)} %broadcast_clamp_fusion.13), kind=kCustom, calls=%fused_computation.2 | custom fusion | bytes 2105344 | tf_op jit(solution)/shard_map/gather | solution.py:18
  116.1 1.8 convert_element_type.116
  117.9 7.0 %gather_fusion.4 = bf16[2048,2,128]{2,1,0:T(2,128)(2,1)S(1)} fusion(bf16[256,2,128]{2,1,0:T(2,128)(2,1)S(1)} %fusion.30, s32[2048]{0:T(1024)S(1)} %broadcast_clamp_fusion.11), kind=kCustom, calls=%fused_computation.4 | custom fusion | bytes 2105344 | tf_op jit(solution)/shard_map/gather | solution.py:18
  125.0 1.8 convert_element_type.119
  126.7 7.1 %gather_fusion.6 = bf16[2048,2,128]{2,1,0:T(2,128)(2,1)S(1)} fusion(bf16[256,2,128]{2,1,0:T(2,128)(2,1)S(1)} %fusion.30, s32[2048]{0:T(1024)S(1)} %broadcast_clamp_fusion.9), kind=kCustom, calls=%fused_computation.6 | custom fusion | bytes 2105344 | tf_op jit(solution)/shard_map/gather | solution.py:18
  133.8 1.8 convert_element_type.122
  135.6 7.0 %gather_fusion.8 = bf16[2048,2,128]{2,1,0:T(2,128)(2,1)S(1)} fusion(bf16[256,2,128]{2,1,0:T(2,128)(2,1)S(1)} %fusion.30, s32[2048]{0:T(1024)S(1)} %broadcast_clamp_fusion.7), kind=kCustom, calls=%fused_computation.8 | custom fusion | bytes 2105344 | tf_op jit(solution)/shard_map/gather | solution.py:18
  142.7 1.7 convert_element_type.125
  144.4 7.1 %gather_fusion.10 = bf16[2048,2,128]{2,1,0:T(2,128)(2,1)S(1)} fusion(bf16[256,2,128]{2,1,0:T(2,128)(2,1)S(1)} %fusion.30, s32[2048]{0:T(1024)S(1)} %broadcast_clamp_fusion.5), kind=kCustom, calls=%fused_computation.10 | custom fusion | bytes 2105344 | tf_op jit(solution)/shard_map/gather | solution.py:18
  153.2 7.1 %gather_fusion.12 = bf16[2048,2,128]{2,1,0:T(2,128)(2,1)S(1)} fusion(bf16[256,2,128]{2,1,0:T(2,128)(2,1)S(1)} %fusion.30, s32[2048]{0:T(1024)S(1)} %broadcast_clamp_fusion.3), kind=kCustom, calls=%fused_computation.12 | custom fusion | bytes 2105344 | tf_op jit(solution)/shard_map/gather | solution.py:18
  162.0 7.0 %gather_fusion.14 = bf16[2048,2,128]{2,1,0:T(2,128)(2,1)S(1)} fusion(bf16[256,2,128]{2,1,0:T(2,128)(2,1)S(1)} %fusion.30, s32[2048]{0:T(1024)S(1)} %broadcast_clamp_fusion.1), kind=kCustom, calls=%fused_computation.14 | custom fusion | bytes 2105344 | tf_op jit(solution)/shard_map/gather | solution.py:18
  169.9 7.0 %gather_fusion.3 = bf16[2048,2,128]{2,1,0:T(2,128)(2,1)S(1)} fusion(bf16[256,2,128]{2,1,0:T(2,128)(2,1)S(1)} %collective-permute-done, s32[2048]{0:T(1024)S(1)} %broadcast_clamp_fusion.12), kind=kCustom, calls=%fused_computation.3 | custom fusion | bytes 2105344 | tf_op jit(solution)/shard_map/gather | solution.py:19
  178.5 3.3 add_convert_fusion.6
  181.8 2.6 pad_maximum_fusion.1
  186.8 2.7 collective-permute-done.1
  189.5 7.0 %gather_fusion.5 = bf16[2048,2,128]{2,1,0:T(2,128)(2,1)S(1)} fusion(bf16[256,2,128]{2,1,0:T(2,128)(2,1)S(1)} %collective-permute-done.1, s32[2048]{0:T(1024)S(1)} %broadcast_clamp_fusion.10), kind=kCustom, calls=%fused_computation.5 | custom fusion | bytes 2105344 | tf_op jit(solution)/shard_map/gather | solution.py:19
  198.1 3.3 add_convert_fusion.5
  201.4 2.4 pad_maximum_fusion.2
  206.3 3.2 collective-permute-done.2
  209.5 7.0 %gather_fusion.7 = bf16[2048,2,128]{2,1,0:T(2,128)(2,1)S(1)} fusion(bf16[256,2,128]{2,1,0:T(2,128)(2,1)S(1)} %collective-permute-done.2, s32[2048]{0:T(1024)S(1)} %broadcast_clamp_fusion.8), kind=kCustom, calls=%fused_computation.7 | custom fusion | bytes 2105344 | tf_op jit(solution)/shard_map/gather | solution.py:19
  218.1 3.3 add_convert_fusion.4
  221.5 2.4 pad_maximum_fusion.3
  225.7 5.3 %collective-permute-done.3 = bf16[256,2,128]{2,1,0:T(2,128)(2,1)S(1)} collective-permute-done((bf16[256,2,128]{2,1,0:T(2,128)(2,1)S(1)}, bf16[256,2,128]{2,1,0:T(2,128)(2,1)S(1)}, u32[]{:S(2)}, u32[]{:S(2)}) %collective-permute-start.3) | collective-permute-done | bytes 131104 | tf_op jit(solution)/shard_map/ppermute | solution.py:14
  231.0 7.4 %gather_fusion.9 = bf16[2048,2,128]{2,1,0:T(2,128)(2,1)S(1)} fusion(bf16[256,2,128]{2,1,0:T(2,128)(2,1)S(1)} %collective-permute-done.3, s32[2048]{0:T(1024)S(1)} %broadcast_clamp_fusion.6), kind=kCustom, calls=%fused_computation.9 | custom fusion | bytes 2105344 | tf_op jit(solution)/shard_map/gather | solution.py:19
  240.1 3.3 add_convert_fusion.3
  243.4 2.4 pad_maximum_fusion.4
  246.9 6.1 %collective-permute-done.4 = bf16[256,2,128]{2,1,0:T(2,128)(2,1)S(1)} collective-permute-done((bf16[256,2,128]{2,1,0:T(2,128)(2,1)S(1)}, bf16[256,2,128]{2,1,0:T(2,128)(2,1)S(1)}, u32[]{:S(2)}, u32[]{:S(2)}) %collective-permute-start.4) | collective-permute-done | bytes 131104 | tf_op jit(solution)/shard_map/ppermute | solution.py:14
  253.0 7.0 %gather_fusion.11 = bf16[2048,2,128]{2,1,0:T(2,128)(2,1)S(1)} fusion(bf16[256,2,128]{2,1,0:T(2,128)(2,1)S(1)} %collective-permute-done.4, s32[2048]{0:T(1024)S(1)} %broadcast_clamp_fusion.4), kind=kCustom, calls=%fused_computation.11 | custom fusion | bytes 2105344 | tf_op jit(solution)/shard_map/gather | solution.py:19
  261.6 3.3 add_convert_fusion.2
  265.0 2.4 pad_maximum_fusion.5
  268.4 6.1 %collective-permute-done.5 = bf16[256,2,128]{2,1,0:T(2,128)(2,1)S(1)} collective-permute-done((bf16[256,2,128]{2,1,0:T(2,128)(2,1)S(1)}, bf16[256,2,128]{2,1,0:T(2,128)(2,1)S(1)}, u32[]{:S(2)}, u32[]{:S(2)}) %collective-permute-start.5) | collective-permute-done | bytes 131104 | tf_op jit(solution)/shard_map/ppermute | solution.py:14
  274.5 7.1 %gather_fusion.13 = bf16[2048,2,128]{2,1,0:T(2,128)(2,1)S(1)} fusion(bf16[256,2,128]{2,1,0:T(2,128)(2,1)S(1)} %collective-permute-done.5, s32[2048]{0:T(1024)S(1)} %broadcast_clamp_fusion.2), kind=kCustom, calls=%fused_computation.13 | custom fusion | bytes 2105344 | tf_op jit(solution)/shard_map/gather | solution.py:19
  283.2 3.3 add_convert_fusion.1
  286.5 2.4 pad_maximum_fusion.6
  290.1 6.1 %collective-permute-done.6 = bf16[256,2,128]{2,1,0:T(2,128)(2,1)S(1)} collective-permute-done((bf16[256,2,128]{2,1,0:T(2,128)(2,1)S(1)}, bf16[256,2,128]{2,1,0:T(2,128)(2,1)S(1)}, u32[]{:S(2)}, u32[]{:S(2)}) %collective-permute-start.6) | collective-permute-done | bytes 131104 | tf_op jit(solution)/shard_map/ppermute | solution.py:14
  296.3 7.0 %gather_fusion.15 = bf16[2048,2,128]{2,1,0:T(2,128)(2,1)S(1)} fusion(bf16[256,2,128]{2,1,0:T(2,128)(2,1)S(1)} %collective-permute-done.6, s32[2048]{0:T(1024)S(1)} %broadcast_clamp_fusion), kind=kCustom, calls=%fused_computation.15 | custom fusion | bytes 2105344 | tf_op jit(solution)/shard_map/gather | solution.py:19
  304.1 3.3 add_convert_fusion
  307.4 2.4 pad_maximum_fusion.7
  310.9 72.5 %all-reduce.2.cloned.1.call-done = f32[64,2,128]{2,0,1:T(8,128)} async-done(((f32[64,2,128]{2,0,1:T(8,128)}), f32[64,2,128]{2,0,1:T(8,128)}) %all-reduce.2.cloned.1.call-update) | async-done | bytes 65552 | tf_op jit(solution)/shard_map/psum | solution.py:61
  384.4 9.5 %fusion.4 = f32[4096,16]{0,1:T(8,128)S(1)} fusion(s32[128]{0:T(128)S(1)} %iota_add_fusion.1, f32[16,2,128]{2,0,1:T(8,128)S(1)} %fusion.40), kind=kOutput, calls=%fused_computation.24 | convolution fusion | flops 108003328 | bytes 270848 | tf_op jit(solution)/shard_map/dot_general | solution.py:30
  393.9 11.2 %convolution_subtract_fusion = f32[4096,16]{0,1:T(8,128)} fusion(f32[4096,16]{0,1:T(8,128)S(1)} %fusion.4, s32[128]{0:T(128)S(1)} %iota_add_fusion.1, f32[16,2,128]{2,0,1:T(8,128)S(1)} %fusion.40), kind=kOutput, calls=%fused_computation.16 | convolution fusion | flops 108068864 | bytes 532992 | tf_op jit(solution)/shard_map/dot_general | solution.py:31
  405.1 110.6 %reduce-scatter.2.cloned.1.call-done = f32[128,16]{0,1:T(8,128)} async-done(((f32[4096,16]{0,1:T(8,128)}), f32[128,16]{0,1:T(8,128)}) %reduce-scatter.2.cloned.1.call-update) | async-done | bytes 8208 | tf_op jit(solution)/shard_map/reduce_scatter | solution.py:70
  (102 shorter events, 35.4 us)
Async XLA Ops:
  6.5 376.8 %all-reduce.2.cloned.1.call-start = ((), (), s32[]{:S(2)}) async-start(), calls=%async_computation.1 | async-start | bytes 131072 | tf_op jit(solution)/shard_map/psum | solution.py:61
  82.5 87.3 %collective-permute-start = (bf16[256,2,128]{2,1,0:T(2,128)(2,1)S(1)}, bf16[256,2,128]{2,1,0:T(2,128)(2,1)S(1)}, u32[]{:S(2)}, u32[]{:S(2)}) collective-permute-start(bf16[256,2,128]{2,1,0:T(2,128)(2,1)S(1)} %fusion.30), channel_id=1, source_target_pairs={{0,32},{32,64},{64,96},{96,128},{128,160},{160,192},{192,224},{224... | collective-permute-start | bytes 393224 | tf_op jit(solution)/shard_map/ppermute | solution.py:14
  92.6 0.8 copy-start.6
  100.6 0.8 copy-start.7
  100.6 1.6 copy-start.13
  176.9 1.6 copy-start.5
  181.8 4.1 copy-start.12
  181.8 4.1 copy-start.14
  184.4 5.0 collective-permute-start.1
  196.5 1.6 copy-start.4
  201.4 3.9 copy-start.11
  201.4 3.9 copy-start.15
  203.9 5.6 %collective-permute-start.2 = (bf16[256,2,128]{2,1,0:T(2,128)(2,1)S(1)}, bf16[256,2,128]{2,1,0:T(2,128)(2,1)S(1)}, u32[]{:S(2)}, u32[]{:S(2)}) collective-permute-start(bf16[256,2,128]{2,1,0:T(2,128)(2,1)S(1)} %collective-permute-done.1), channel_id=1, source_target_pairs={{0,32},{32,64},{64,96},{96,128},{128,160},{160,192},{192,224},{224... | collective-permute-start | bytes 393224 | tf_op jit(solution)/shard_map/ppermute | solution.py:14
  216.6 1.6 copy-start.3
  221.4 3.4 copy-start.10
  221.4 3.4 copy-start.16
  223.9 7.1 %collective-permute-start.3 = (bf16[256,2,128]{2,1,0:T(2,128)(2,1)S(1)}, bf16[256,2,128]{2,1,0:T(2,128)(2,1)S(1)}, u32[]{:S(2)}, u32[]{:S(2)}) collective-permute-start(bf16[256,2,128]{2,1,0:T(2,128)(2,1)S(1)} %collective-permute-done.2), channel_id=1, source_target_pairs={{0,32},{32,64},{64,96},{96,128},{128,160},{160,192},{192,224},{224... | collective-permute-start | bytes 393224 | tf_op jit(solution)/shard_map/ppermute | solution.py:14
  238.5 1.6 copy-start.2
  243.4 2.6 copy-start.9
  243.4 2.6 copy-start.17
  245.8 7.2 %collective-permute-start.4 = (bf16[256,2,128]{2,1,0:T(2,128)(2,1)S(1)}, bf16[256,2,128]{2,1,0:T(2,128)(2,1)S(1)}, u32[]{:S(2)}, u32[]{:S(2)}) collective-permute-start(bf16[256,2,128]{2,1,0:T(2,128)(2,1)S(1)} %collective-permute-done.3), channel_id=1, source_target_pairs={{0,32},{32,64},{64,96},{96,128},{128,160},{160,192},{192,224},{224... | collective-permute-start | bytes 393224 | tf_op jit(solution)/shard_map/ppermute | solution.py:14
  260.0 1.6 copy-start.1
  264.9 2.6 copy-start.8
  264.9 2.6 copy-start.18
  267.4 7.2 %collective-permute-start.5 = (bf16[256,2,128]{2,1,0:T(2,128)(2,1)S(1)}, bf16[256,2,128]{2,1,0:T(2,128)(2,1)S(1)}, u32[]{:S(2)}, u32[]{:S(2)}) collective-permute-start(bf16[256,2,128]{2,1,0:T(2,128)(2,1)S(1)} %collective-permute-done.4), channel_id=1, source_target_pairs={{0,32},{32,64},{64,96},{96,128},{128,160},{160,192},{192,224},{224... | collective-permute-start | bytes 393224 | tf_op jit(solution)/shard_map/ppermute | solution.py:14
  281.6 1.6 copy-start
  286.5 2.7 copy-start.19
  288.9 7.3 %collective-permute-start.6 = (bf16[256,2,128]{2,1,0:T(2,128)(2,1)S(1)}, bf16[256,2,128]{2,1,0:T(2,128)(2,1)S(1)}, u32[]{:S(2)}, u32[]{:S(2)}) collective-permute-start(bf16[256,2,128]{2,1,0:T(2,128)(2,1)S(1)} %collective-permute-done.5), channel_id=1, source_target_pairs={{0,32},{32,64},{64,96},{96,128},{128,160},{160,192},{192,224},{224... | collective-permute-start | bytes 393224 | tf_op jit(solution)/shard_map/ppermute | solution.py:14
  307.4 2.5 copy-start.20
  310.8 205.0 %reduce-scatter.2.cloned.1.call-start = ((), (), s32[]{:S(2)}) async-start(), calls=%async_computation.2 | async-start | bytes 270336 | tf_op jit(solution)/shard_map/reduce_scatter | solution.py:70
Sparse Core Ops, SparseCore 0:
  310.9 72.3 all-reduce.1
  405.3 110.4 reduce-scatter.1
where the time goes:
time: 534 us; the launch traced here: 524 us
  waiting for transfers between devices  213 us (40%)
  local copies, waits for them, and re-layouts  119 us (22%)
  blocking collectives  72.8 us (14%)
  other arithmetic  70.4 us (13%)
  matrix products  28.5 us (5%)
  between operations  14.4 us (3%)
  starting transfers between devices  5.95 us (1%)
    reduce_scatter x1, waiting for transfers between devices, on_device(): lax.psum_scatter(lag_block(lag_rows, freq_rows, owned), 'freq', scatter_d...  111 us
    psum x1, blocking collectives, on_device(): power = lax.psum(jnp.sum(values * values, axis=(1, 2)), 'freq')  72.8 us
    psum x1, waiting for transfers between devices, on_device(): totals = lax.psum(partial_stack, 'blk')  72.5 us
    gather x8, local copies, waits for them, and re-layouts, cross_stack(): right = remote[second_rows].astype(jnp.float32)  56.8 us
    gather x8, local copies, waits for them, and re-layouts, cross_stack(): left = white[first_rows].astype(jnp.float32)  56.4 us
    ppermute x7, waiting for transfers between devices, from_behind(): lax.ppermute(x, axis, [(i, (i + by) % devices) for i in range(devices)])  29.6 us
    another operation x8, other arithmetic  26.3 us
    another operation x8, other arithmetic, cross_stack(): cross = jnp.stack([real_part, imag_part], 1).astype(jnp.bfloat16)  19.6 us
  transfers between devices with their start and end apart: 9, of which 8 were waited for; matrix products, arithmetic and copies ran while one was open for 17% of the time, Pallas kernels for 0%

commit v1 on v0

--- a/solution.py
+++ b/solution.py
@@ -35,7 +35,7 @@
     blocks = lax.axis_size("blk")
     freq_dev = spectra.shape[2]
     values = spectra.astype(jnp.float32)
-    power = lax.psum(jnp.sum(values * values, axis=(1, 2)), "freq")
+    power = jnp.sum(lax.all_gather(jnp.sum(values * values, axis=(1, 2)), "freq"), axis=0)
     rms = jnp.sqrt(power / (2 * F) + 1e-06)
     white = (values / rms[:, None, None]).astype(jnp.bfloat16)
     total = jnp.zeros((NB, 2 * freq_dev), jnp.float32)

time: 534 us -> 500 us (0.936); the launches traced: 524 us -> 497 us
  blocking collectives: 72.8 us -> 44.8 us
    psum x1 -> x0, blocking collectives: 72.8 us -> none  [on_device(): power = lax.psum(jnp.sum(values * values, axis=(1, 2)), 'freq')]
    all_gather x0 -> x1, blocking collectives: none -> 44.8 us  [on_device(): lax.all_gather(jnp.sum(values * values, axis=(1, 2)), 'freq')]
  transfers between devices with their start and end apart: 9 -> 9, of which waited for: 8 -> 8; matrix products, arithmetic and copies ran while one was open for 17% -> 18% of each run, Pallas kernels for 0% -> 0%
where the time goes in v1:
time: 500 us; the launch traced here: 497 us
  waiting for transfers between devices  214 us (43%)
  local copies, waits for them, and re-layouts  119 us (24%)
  other arithmetic  70.4 us (14%)
  blocking collectives  44.8 us (9%)
  matrix products  28.5 us (6%)
  between operations  14.4 us (3%)
  starting transfers between devices  6.1 us (1%)
    reduce_scatter x1, waiting for transfers between devices, on_device(): lax.psum_scatter(lag_block(lag_rows, freq_rows, owned), 'freq', scatter_d...  111 us
    psum x1, waiting for transfers between devices, on_device(): totals = lax.psum(partial_stack, 'blk')  72.4 us
    gather x8, local copies, waits for them, and re-layouts, cross_stack(): right = remote[second_rows].astype(jnp.float32)  56.8 us
    gather x8, local copies, waits for them, and re-layouts, cross_stack(): left = white[first_rows].astype(jnp.float32)  56.4 us
    all_gather x1, blocking collectives, on_device(): lax.all_gather(jnp.sum(values * values, axis=(1, 2)), 'freq')  44.8 us
    ppermute x7, waiting for transfers between devices, from_behind(): lax.ppermute(x, axis, [(i, (i + by) % devices) for i in range(devices)])  30.4 us
    another operation x8, other arithmetic  26.3 us
    another operation x8, other arithmetic, cross_stack(): cross = jnp.stack([real_part, imag_part], 1).astype(jnp.bfloat16)  19.6 us
  transfers between devices with their start and end apart: 9, of which 8 were waited for; matrix products, arithmetic and copies ran while one was open for 18% of the time, Pallas kernels for 0%

profile of v1, /device:TPU:8, one launch (start us, length us, event | category | flops | bytes accessed | tf_op | source)
XLA Modules:
  0.0 497.1 jit_solution(13551304964917014355)
XLA Ops:
  6.5 1.9 fusion.29
  8.5 44.8 %all-gather.1 = f32[32,1,256]{2,1,0:T(1,128)S(1)} all-gather(f32[1,1,256]{2,1,0:T(1,128)S(1)} %bitcast.137), channel_id=2, replica_groups=mesh['blk'=8,'freq'=32] {'freq'}, dimensions={0}, use_global_device_ids=true | all-gather | bytes 33792 | tf_op jit(solution)/shard_map/all_gather | solution.py:38
  54.6 2.1 collective-permute-start
  58.0 7.1 %gather_fusion = bf16[2048,2,128]{2,1,0:T(2,128)(2,1)S(1)} fusion(bf16[256,2,128]{2,1,0:T(2,128)(2,1)S(1)} %fusion.30, s32[2048]{0:T(1024)S(1)} %broadcast_clamp_fusion.15), kind=kCustom, calls=%fused_computation | custom fusion | bytes 2105344 | tf_op jit(solution)/shard_map/gather | solution.py:18
  66.0 7.0 %gather_fusion.1 = bf16[2048,2,128]{2,1,0:T(2,128)(2,1)S(1)} fusion(bf16[256,2,128]{2,1,0:T(2,128)(2,1)S(1)} %fusion.30, s32[2048]{0:T(1024)S(1)} %broadcast_clamp_fusion.14), kind=kCustom, calls=%fused_computation.1 | custom fusion | bytes 2105344 | tf_op jit(solution)/shard_map/gather | solution.py:19
  74.9 3.3 add_convert_fusion.7
  78.2 2.4 pad_maximum_fusion
  81.6 7.0 %gather_fusion.2 = bf16[2048,2,128]{2,1,0:T(2,128)(2,1)S(1)} fusion(bf16[256,2,128]{2,1,0:T(2,128)(2,1)S(1)} %fusion.30, s32[2048]{0:T(1024)S(1)} %broadcast_clamp_fusion.13), kind=kCustom, calls=%fused_computation.2 | custom fusion | bytes 2105344 | tf_op jit(solution)/shard_map/gather | solution.py:18
  88.7 1.8 convert_element_type.116
  90.4 7.0 %gather_fusion.4 = bf16[2048,2,128]{2,1,0:T(2,128)(2,1)S(1)} fusion(bf16[256,2,128]{2,1,0:T(2,128)(2,1)S(1)} %fusion.30, s32[2048]{0:T(1024)S(1)} %broadcast_clamp_fusion.11), kind=kCustom, calls=%fused_computation.4 | custom fusion | bytes 2105344 | tf_op jit(solution)/shard_map/gather | solution.py:18
  97.5 1.8 convert_element_type.119
  99.2 7.1 %gather_fusion.6 = bf16[2048,2,128]{2,1,0:T(2,128)(2,1)S(1)} fusion(bf16[256,2,128]{2,1,0:T(2,128)(2,1)S(1)} %fusion.30, s32[2048]{0:T(1024)S(1)} %broadcast_clamp_fusion.9), kind=kCustom, calls=%fused_computation.6 | custom fusion | bytes 2105344 | tf_op jit(solution)/shard_map/gather | solution.py:18
  106.3 1.8 convert_element_type.122
  108.1 7.0 %gather_fusion.8 = bf16[2048,2,128]{2,1,0:T(2,128)(2,1)S(1)} fusion(bf16[256,2,128]{2,1,0:T(2,128)(2,1)S(1)} %fusion.30, s32[2048]{0:T(1024)S(1)} %broadcast_clamp_fusion.7), kind=kCustom, calls=%fused_computation.8 | custom fusion | bytes 2105344 | tf_op jit(solution)/shard_map/gather | solution.py:18
  116.9 7.1 %gather_fusion.10 = bf16[2048,2,128]{2,1,0:T(2,128)(2,1)S(1)} fusion(bf16[256,2,128]{2,1,0:T(2,128)(2,1)S(1)} %fusion.30, s32[2048]{0:T(1024)S(1)} %broadcast_clamp_fusion.5), kind=kCustom, calls=%fused_computation.10 | custom fusion | bytes 2105344 | tf_op jit(solution)/shard_map/gather | solution.py:18
  125.7 7.1 %gather_fusion.12 = bf16[2048,2,128]{2,1,0:T(2,128)(2,1)S(1)} fusion(bf16[256,2,128]{2,1,0:T(2,128)(2,1)S(1)} %fusion.30, s32[2048]{0:T(1024)S(1)} %broadcast_clamp_fusion.3), kind=kCustom, calls=%fused_computation.12 | custom fusion | bytes 2105344 | tf_op jit(solution)/shard_map/gather | solution.py:18
  134.5 7.0 %gather_fusion.14 = bf16[2048,2,128]{2,1,0:T(2,128)(2,1)S(1)} fusion(bf16[256,2,128]{2,1,0:T(2,128)(2,1)S(1)} %fusion.30, s32[2048]{0:T(1024)S(1)} %broadcast_clamp_fusion.1), kind=kCustom, calls=%fused_computation.14 | custom fusion | bytes 2105344 | tf_op jit(solution)/shard_map/gather | solution.py:18
  142.4 7.0 %gather_fusion.3 = bf16[2048,2,128]{2,1,0:T(2,128)(2,1)S(1)} fusion(bf16[256,2,128]{2,1,0:T(2,128)(2,1)S(1)} %collective-permute-done, s32[2048]{0:T(1024)S(1)} %broadcast_clamp_fusion.12), kind=kCustom, calls=%fused_computation.3 | custom fusion | bytes 2105344 | tf_op jit(solution)/shard_map/gather | solution.py:19
  151.0 3.3 add_convert_fusion.6
  154.3 2.6 pad_maximum_fusion.1
  159.2 3.3 collective-permute-done.1
  162.5 7.0 %gather_fusion.5 = bf16[2048,2,128]{2,1,0:T(2,128)(2,1)S(1)} fusion(bf16[256,2,128]{2,1,0:T(2,128)(2,1)S(1)} %collective-permute-done.1, s32[2048]{0:T(1024)S(1)} %broadcast_clamp_fusion.10), kind=kCustom, calls=%fused_computation.5 | custom fusion | bytes 2105344 | tf_op jit(solution)/shard_map/gather | solution.py:19
  171.1 3.3 add_convert_fusion.5
  174.5 2.4 pad_maximum_fusion.2
  179.2 3.3 collective-permute-done.2
  182.5 7.0 %gather_fusion.7 = bf16[2048,2,128]{2,1,0:T(2,128)(2,1)S(1)} fusion(bf16[256,2,128]{2,1,0:T(2,128)(2,1)S(1)} %collective-permute-done.2, s32[2048]{0:T(1024)S(1)} %broadcast_clamp_fusion.8), kind=kCustom, calls=%fused_computation.7 | custom fusion | bytes 2105344 | tf_op jit(solution)/shard_map/gather | solution.py:19
  191.2 3.3 add_convert_fusion.4
  194.5 2.4 pad_maximum_fusion.3
  198.6 5.4 %collective-permute-done.3 = bf16[256,2,128]{2,1,0:T(2,128)(2,1)S(1)} collective-permute-done((bf16[256,2,128]{2,1,0:T(2,128)(2,1)S(1)}, bf16[256,2,128]{2,1,0:T(2,128)(2,1)S(1)}, u32[]{:S(2)}, u32[]{:S(2)}) %collective-permute-start.3) | collective-permute-done | bytes 131104 | tf_op jit(solution)/shard_map/ppermute | solution.py:14
  204.1 7.4 %gather_fusion.9 = bf16[2048,2,128]{2,1,0:T(2,128)(2,1)S(1)} fusion(bf16[256,2,128]{2,1,0:T(2,128)(2,1)S(1)} %collective-permute-done.3, s32[2048]{0:T(1024)S(1)} %broadcast_clamp_fusion.6), kind=kCustom, calls=%fused_computation.9 | custom fusion | bytes 2105344 | tf_op jit(solution)/shard_map/gather | solution.py:19
  213.1 3.3 add_convert_fusion.3
  216.4 2.4 pad_maximum_fusion.4
  219.9 6.1 %collective-permute-done.4 = bf16[256,2,128]{2,1,0:T(2,128)(2,1)S(1)} collective-permute-done((bf16[256,2,128]{2,1,0:T(2,128)(2,1)S(1)}, bf16[256,2,128]{2,1,0:T(2,128)(2,1)S(1)}, u32[]{:S(2)}, u32[]{:S(2)}) %collective-permute-start.4) | collective-permute-done | bytes 131104 | tf_op jit(solution)/shard_map/ppermute | solution.py:14
  226.0 7.0 %gather_fusion.11 = bf16[2048,2,128]{2,1,0:T(2,128)(2,1)S(1)} fusion(bf16[256,2,128]{2,1,0:T(2,128)(2,1)S(1)} %collective-permute-done.4, s32[2048]{0:T(1024)S(1)} %broadcast_clamp_fusion.4), kind=kCustom, calls=%fused_computation.11 | custom fusion | bytes 2105344 | tf_op jit(solution)/shard_map/gather | solution.py:19
  234.6 3.3 add_convert_fusion.2
  238.0 2.4 pad_maximum_fusion.5
  241.4 6.1 %collective-permute-done.5 = bf16[256,2,128]{2,1,0:T(2,128)(2,1)S(1)} collective-permute-done((bf16[256,2,128]{2,1,0:T(2,128)(2,1)S(1)}, bf16[256,2,128]{2,1,0:T(2,128)(2,1)S(1)}, u32[]{:S(2)}, u32[]{:S(2)}) %collective-permute-start.5) | collective-permute-done | bytes 131104 | tf_op jit(solution)/shard_map/ppermute | solution.py:14
  247.6 7.1 %gather_fusion.13 = bf16[2048,2,128]{2,1,0:T(2,128)(2,1)S(1)} fusion(bf16[256,2,128]{2,1,0:T(2,128)(2,1)S(1)} %collective-permute-done.5, s32[2048]{0:T(1024)S(1)} %broadcast_clamp_fusion.2), kind=kCustom, calls=%fused_computation.13 | custom fusion | bytes 2105344 | tf_op jit(solution)/shard_map/gather | solution.py:19
  256.2 3.3 add_convert_fusion.1
  259.5 2.4 pad_maximum_fusion.6
  263.2 6.1 %collective-permute-done.6 = bf16[256,2,128]{2,1,0:T(2,128)(2,1)S(1)} collective-permute-done((bf16[256,2,128]{2,1,0:T(2,128)(2,1)S(1)}, bf16[256,2,128]{2,1,0:T(2,128)(2,1)S(1)}, u32[]{:S(2)}, u32[]{:S(2)}) %collective-permute-start.6) | collective-permute-done | bytes 131104 | tf_op jit(solution)/shard_map/ppermute | solution.py:14
  269.3 7.0 %gather_fusion.15 = bf16[2048,2,128]{2,1,0:T(2,128)(2,1)S(1)} fusion(bf16[256,2,128]{2,1,0:T(2,128)(2,1)S(1)} %collective-permute-done.6, s32[2048]{0:T(1024)S(1)} %broadcast_clamp_fusion), kind=kCustom, calls=%fused_computation.15 | custom fusion | bytes 2105344 | tf_op jit(solution)/shard_map/gather | solution.py:19
  277.1 3.3 add_convert_fusion
  280.4 2.4 pad_maximum_fusion.7
  283.9 72.4 %all-reduce.2.cloned.1.call-done = f32[64,2,128]{2,0,1:T(8,128)} async-done(((f32[64,2,128]{2,0,1:T(8,128)}), f32[64,2,128]{2,0,1:T(8,128)}) %all-reduce.2.cloned.1.call-update) | async-done | bytes 65552 | tf_op jit(solution)/shard_map/psum | solution.py:61
  357.4 9.5 %fusion.4 = f32[4096,16]{0,1:T(8,128)S(1)} fusion(s32[128]{0:T(128)S(1)} %iota_add_fusion.1, f32[16,2,128]{2,0,1:T(8,128)S(1)} %fusion.40), kind=kOutput, calls=%fused_computation.24 | convolution fusion | flops 108003328 | bytes 270848 | tf_op jit(solution)/shard_map/dot_general | solution.py:30
  366.9 11.2 %convolution_subtract_fusion = f32[4096,16]{0,1:T(8,128)} fusion(f32[4096,16]{0,1:T(8,128)S(1)} %fusion.4, s32[128]{0:T(128)S(1)} %iota_add_fusion.1, f32[16,2,128]{2,0,1:T(8,128)S(1)} %fusion.40), kind=kOutput, calls=%fused_computation.16 | convolution fusion | flops 108068864 | bytes 532992 | tf_op jit(solution)/shard_map/dot_general | solution.py:31
  378.1 110.6 %reduce-scatter.2.cloned.1.call-done = f32[128,16]{0,1:T(8,128)} async-done(((f32[4096,16]{0,1:T(8,128)}), f32[128,16]{0,1:T(8,128)}) %reduce-scatter.2.cloned.1.call-update) | async-done | bytes 8208 | tf_op jit(solution)/shard_map/reduce_scatter | solution.py:70
  (103 shorter events, 35.2 us)
Async XLA Ops:
  6.5 349.8 %all-reduce.2.cloned.1.call-start = ((), (), s32[]{:S(2)}) async-start(), calls=%async_computation.1 | async-start | bytes 131072 | tf_op jit(solution)/shard_map/psum | solution.py:61
  54.6 87.8 %collective-permute-start = (bf16[256,2,128]{2,1,0:T(2,128)(2,1)S(1)}, bf16[256,2,128]{2,1,0:T(2,128)(2,1)S(1)}, u32[]{:S(2)}, u32[]{:S(2)}) collective-permute-start(bf16[256,2,128]{2,1,0:T(2,128)(2,1)S(1)} %fusion.30), channel_id=1, source_target_pairs={{0,32},{32,64},{64,96},{96,128},{128,160},{160,192},{192,224},{224... | collective-permute-start | bytes 393224 | tf_op jit(solution)/shard_map/ppermute | solution.py:14
  65.1 0.8 copy-start.6
  73.1 0.8 copy-start.7
  73.1 1.6 copy-start.13
  149.4 1.6 copy-start.5
  154.3 4.0 copy-start.12
  154.3 4.0 copy-start.14
  157.0 5.5 %collective-permute-start.1 = (bf16[256,2,128]{2,1,0:T(2,128)(2,1)S(1)}, bf16[256,2,128]{2,1,0:T(2,128)(2,1)S(1)}, u32[]{:S(2)}, u32[]{:S(2)}) collective-permute-start(bf16[256,2,128]{2,1,0:T(2,128)(2,1)S(1)} %collective-permute-done), channel_id=1, source_target_pairs={{0,32},{32,64},{64,96},{96,128},{128,160},{160,192},{192,224},{224... | collective-permute-start | bytes 393224 | tf_op jit(solution)/shard_map/ppermute | solution.py:14
  169.6 1.6 copy-start.4
  174.4 3.8 copy-start.11
  174.4 3.8 copy-start.15
  176.9 5.6 %collective-permute-start.2 = (bf16[256,2,128]{2,1,0:T(2,128)(2,1)S(1)}, bf16[256,2,128]{2,1,0:T(2,128)(2,1)S(1)}, u32[]{:S(2)}, u32[]{:S(2)}) collective-permute-start(bf16[256,2,128]{2,1,0:T(2,128)(2,1)S(1)} %collective-permute-done.1), channel_id=1, source_target_pairs={{0,32},{32,64},{64,96},{96,128},{128,160},{160,192},{192,224},{224... | collective-permute-start | bytes 393224 | tf_op jit(solution)/shard_map/ppermute | solution.py:14
  189.6 1.6 copy-start.3
  194.5 3.3 copy-start.10
  194.5 3.3 copy-start.16
  196.9 7.1 %collective-permute-start.3 = (bf16[256,2,128]{2,1,0:T(2,128)(2,1)S(1)}, bf16[256,2,128]{2,1,0:T(2,128)(2,1)S(1)}, u32[]{:S(2)}, u32[]{:S(2)}) collective-permute-start(bf16[256,2,128]{2,1,0:T(2,128)(2,1)S(1)} %collective-permute-done.2), channel_id=1, source_target_pairs={{0,32},{32,64},{64,96},{96,128},{128,160},{160,192},{192,224},{224... | collective-permute-start | bytes 393224 | tf_op jit(solution)/shard_map/ppermute | solution.py:14
  211.5 1.6 copy-start.2
  216.4 2.6 copy-start.9
  216.4 2.6 copy-start.17
  218.8 7.2 %collective-permute-start.4 = (bf16[256,2,128]{2,1,0:T(2,128)(2,1)S(1)}, bf16[256,2,128]{2,1,0:T(2,128)(2,1)S(1)}, u32[]{:S(2)}, u32[]{:S(2)}) collective-permute-start(bf16[256,2,128]{2,1,0:T(2,128)(2,1)S(1)} %collective-permute-done.3), channel_id=1, source_target_pairs={{0,32},{32,64},{64,96},{96,128},{128,160},{160,192},{192,224},{224... | collective-permute-start | bytes 393224 | tf_op jit(solution)/shard_map/ppermute | solution.py:14
  233.1 1.6 copy-start.1
  237.9 2.6 copy-start.8
  238.0 2.6 copy-start.18
  240.4 7.2 %collective-permute-start.5 = (bf16[256,2,128]{2,1,0:T(2,128)(2,1)S(1)}, bf16[256,2,128]{2,1,0:T(2,128)(2,1)S(1)}, u32[]{:S(2)}, u32[]{:S(2)}) collective-permute-start(bf16[256,2,128]{2,1,0:T(2,128)(2,1)S(1)} %collective-permute-done.4), channel_id=1, source_target_pairs={{0,32},{32,64},{64,96},{96,128},{128,160},{160,192},{192,224},{224... | collective-permute-start | bytes 393224 | tf_op jit(solution)/shard_map/ppermute | solution.py:14
  254.6 1.6 copy-start
  259.5 2.7 copy-start.19
  262.0 7.3 %collective-permute-start.6 = (bf16[256,2,128]{2,1,0:T(2,128)(2,1)S(1)}, bf16[256,2,128]{2,1,0:T(2,128)(2,1)S(1)}, u32[]{:S(2)}, u32[]{:S(2)}) collective-permute-start(bf16[256,2,128]{2,1,0:T(2,128)(2,1)S(1)} %collective-permute-done.5), channel_id=1, source_target_pairs={{0,32},{32,64},{64,96},{96,128},{128,160},{160,192},{192,224},{224... | collective-permute-start | bytes 393224 | tf_op jit(solution)/shard_map/ppermute | solution.py:14
  280.4 2.5 copy-start.20
  283.8 204.9 %reduce-scatter.2.cloned.1.call-start = ((), (), s32[]{:S(2)}) async-start(), calls=%async_computation.2 | async-start | bytes 270336 | tf_op jit(solution)/shard_map/reduce_scatter | solution.py:70
Sparse Core Ops, SparseCore 0:
  284.0 72.3 all-reduce.1
  378.3 110.4 reduce-scatter.1
